TPU v7x, 32 devices: a whole 2x2x4 slice. The times are simulated.
32 devices in a mesh: row: 8 (over z, y), col: 4 (over x, core).
Axes of the slice: x: 2, y: 2, z: 4, core: 2. Of those that a mesh axis runs over, the one named last changes fastest.
Arguments:
- amplitudes: float32 [64, 2, 640], P('row', None, 'col'), may hold values from -6 to 6
- integrals: float32 [2, 640, 640, 640], P(None, 'col', 'row'), may hold values from -0.5 to 0.5
- virt_irrep: int32 [640], replicated, may hold values from 0 to 7
- pair_irrep: int32 [64], replicated, may hold values from 0 to 7
- tile_mask: int32 [8, 8], replicated, may hold values 0 or 1
Outputs:
- residual: float32 [64, 640, 640], P('col', 'row')
All inputs are finite; a program needn't handle non-finite values.
Results may differ from a plain program's by a relative error of at most 0.000071.
Values sent between devices are 32-bit elements; how exact they have to be, the bound alone decides.
A program may use at most 192 MiB of HBM per device.

v0:
```python
import jax
import jax.numpy as jnp
from jax import lax
from jax.sharding import PartitionSpec as P


def reduce_pairs(partial_sums):
    return lax.psum_scatter(partial_sums, "col", scatter_dimension=0, tiled=True)


def mirror_after(owned):
    swapped = lax.all_to_all(owned, "row", split_axis=2, concat_axis=1, tiled=True)
    return owned - jnp.transpose(swapped, (0, 2, 1))


def mask_slab(amps, c_labels, d_labels, pair_irrep, tile_mask):
    labels_range = jnp.arange(tile_mask.shape[0], dtype=jnp.int32)
    c_onehot = (c_labels[:, None] == labels_range[None, :]).astype(jnp.float32)
    d_onehot = (d_labels[:, None] == labels_range[None, :]).astype(jnp.float32)
    tile_float = tile_mask.astype(jnp.float32)
    screen = jnp.dot(
        jnp.dot(
            c_onehot,
            tile_float,
            precision=lax.Precision.HIGHEST,
            preferred_element_type=jnp.float32,
        ),
        d_onehot.T,
        precision=lax.Precision.HIGHEST,
        preferred_element_type=jnp.float32,
    )
    allowed = (
        jnp.bitwise_xor(c_labels[:, None], d_labels[None, :])[None, :, :]
        == pair_irrep[:, None, None]
    )
    return amps * screen[None, :, :] * allowed.astype(jnp.float32)


def local(amplitudes, integrals, virt_irrep, pair_irrep, tile_mask):
    slab_width = amplitudes.shape[1]
    d_width = integrals.shape[1]
    a_width = integrals.shape[2]
    full_width = integrals.shape[3]
    row_index = lax.axis_index("row")
    col_index = lax.axis_index("col")
    gathered = lax.all_gather(amplitudes, "row", axis=0, tiled=True)
    pair_count = gathered.shape[0]
    c_labels = virt_irrep[:slab_width]
    d_labels = lax.dynamic_slice_in_dim(virt_irrep, col_index * d_width, d_width)
    masked = mask_slab(gathered, c_labels, d_labels, pair_irrep, tile_mask)
    partial_sums = jnp.dot(
        masked.reshape(pair_count, slab_width * d_width),
        integrals.reshape(slab_width * d_width, a_width * full_width),
        precision=lax.Precision.HIGHEST,
        preferred_element_type=jnp.float32,
    ).reshape(pair_count, a_width, full_width)
    mirrored = mirror_after(reduce_pairs(partial_sums))
    own_pairs = mirrored.shape[0]
    a_labels = lax.dynamic_slice_in_dim(virt_irrep, row_index * a_width, a_width)
    pair_labels = lax.dynamic_slice_in_dim(pair_irrep, col_index * own_pairs, own_pairs)
    kept_mask = (
        jnp.bitwise_xor(a_labels[:, None], virt_irrep[None, :])[None, :, :]
        == pair_labels[:, None, None]
    )
    return mirrored * kept_mask.astype(jnp.float32)


def solution(mesh):
    in_specs = (P("row", None, "col"), P(None, "col", "row", None), P(), P(), P())
    out_specs = P("col", "row", None)
    return jax.shard_map(local, mesh=mesh, in_specs=in_specs, out_specs=out_specs, check_vma=False)
```

profile of v0, /device:TPU:0, one launch (start us, length us, event | category | flops | bytes accessed | tf_op | source)
XLA Modules:
  0.0 375.9 jit_solution(2555133089651261318)
XLA Ops:
  6.5 0.0 reduce-scatter.2.cloned.1.call-start
  6.5 0.7 slice.3
  7.2 0.8 dynamic_slice.11
  8.0 0.9 fusion.6
  8.9 0.1 broadcast_xor_fusion.1
  8.9 0.2 fusion.4
  9.1 32.6 %all_gather.3 = f32[64,2,160]{2,1,0:T(2,128)S(1)} all-gather(f32[8,2,160]{2,1,0:T(2,128)} %param.5), channel_id=1, replica_groups=mesh['row'=8,'col'=4] {'row'}, dimensions={0}, use_global_device_ids=true | all-gather | bytes 92160 | tf_op jit(solution)/shard_map/all_gather | solution.py:46
  41.7 0.8 compare_select_fusion
  42.5 0.1 reshape.68
  42.7 79.4 %fusion = f32[64,80,640]{2,0,1:T(8,128)} fusion(f32[64,320,1]{1,0,2:T(8,128)S(1)} %reshape.68, f32[40,8,80,640]{3,2,1,0:T(8,128)} %bitcast.26), kind=kOutput, calls=%fused_computation | convolution fusion | flops 12582912000 | bytes 78725120 | tf_op jit(solution)/shard_map/dot_general | solution.py:51
  122.1 0.0 reduce-scatter.2.cloned.1.call-update
  122.2 101.4 %reduce-scatter.2.cloned.1.call-done = f32[16,80,640]{2,0,1:T(8,128)} async-done(((f32[64,80,640]{2,0,1:T(8,128)}), f32[16,80,640]{2,0,1:T(8,128)}) %reduce-scatter.2.cloned.1.call-update) | async-done | bytes 3276816 | tf_op jit(solution)/shard_map/reduce_scatter | solution.py:8
  223.6 5.6 %copy.16 = f32[16,80,640]{1,0,2:T(8,128)} copy(f32[16,80,640]{2,0,1:T(8,128)} %reduce-scatter.2.cloned.1.call-done) | data formatting | bytes 6553600 | tf_op jit(solution)/shard_map/reduce_scatter | solution.py:8
  229.2 0.0 copy-start.2
  229.2 0.0 copy-start.1
  229.2 5.6 %all-to-all-start = ((f32[16,80,640]{1,0,2:T(8,128)}), f32[16,80,640]{1,0,2:T(8,128)}, u32[]{:S(2)}, u32[]{:S(2)}) async-start(f32[16,80,640]{1,0,2:T(8,128)} %copy.16), calls=%async_computation.1 | async-start | bytes 10485760 | tf_op jit(solution)/shard_map/all_to_all | solution.py:12
  234.8 0.0 copy-done.2
  234.9 0.1 dynamic_slice.10
  234.9 0.0 copy-done.1
  234.9 0.1 dynamic_slice.9
  235.0 0.1 broadcast_xor_fusion
  235.1 115.3 %all-to-all-done = f32[16,80,640]{1,0,2:T(8,128)} async-done(((f32[16,80,640]{1,0,2:T(8,128)}), f32[16,80,640]{1,0,2:T(8,128)}, u32[]{:S(2)}, u32[]{:S(2)}) %all-to-all-start) | async-done | bytes 3276832 | tf_op jit(solution)/shard_map/all_to_all | solution.py:12
  350.4 7.9 %copy.29 = f32[16,80,8,80]{1,2,0,3:T(8,128)} copy(f32[16,80,8,80]{1,0,3,2:T(8,128)} %bitcast.1) | data formatting | bytes 6553600 | tf_op jit(solution)/shard_map/all_to_all | solution.py:12
  358.3 0.0 copy-start
  358.3 5.5 %all_to_all.16 = f32[16,640,80]{1,0,2:T(8,128)} reshape(f32[16,8,80,80]{2,1,0,3:T(8,128)} %bitcast.27) | data formatting | bytes 6553600 | tf_op jit(solution)/shard_map/all_to_all | solution.py:12
  363.8 0.0 copy-done
  363.8 2.5 fusion.3
  366.4 2.7 copy.18
Async XLA Ops:
  6.5 217.0 %reduce-scatter.2.cloned.1.call-start = ((), (), s32[]{:S(2)}) async-start(), calls=%async_computation.2 | async-start | bytes 16384000 | tf_op jit(solution)/shard_map/reduce_scatter | solution.py:8
  229.2 5.6 %copy-start.2 = (s32[64]{0:T(128)S(1)}, s32[64]{0:T(128)}, u32[]{:S(2)}) copy-start(s32[64]{0:T(128)} %param.8) | copy-start | bytes 772
  229.2 5.7 %copy-start.1 = (s32[640]{0:T(1024)S(1)}, s32[640]{0:T(1024)}, u32[]{:S(2)}) copy-start(s32[640]{0:T(1024)} %param.7) | copy-start | bytes 7684
  229.2 121.2 %all-to-all-start = ((f32[16,80,640]{1,0,2:T(8,128)}), f32[16,80,640]{1,0,2:T(8,128)}, u32[]{:S(2)}, u32[]{:S(2)}) async-start(f32[16,80,640]{1,0,2:T(8,128)} %copy.16), calls=%async_computation.1 | async-start | bytes 10485760 | tf_op jit(solution)/shard_map/all_to_all | solution.py:12
  358.3 5.5 %copy-start = (f32[16,80,640]{2,0,1:T(8,128)S(1)}, f32[16,80,640]{2,0,1:T(8,128)}, u32[]{:S(2)}) copy-start(f32[16,80,640]{2,0,1:T(8,128)} %reduce-scatter.2.cloned.1.call-done) | copy-start | bytes 9830404
Sparse Core Ops, SparseCore 0:
  122.3 101.2 reduce-scatter.1
where the time goes:
time: 376 us
  waiting for transfers between devices  217 us (58%)
  matrix products  80.5 us (21%)
  blocking collectives  32.6 us (9%)
  local copies, waits for them, and re-layouts  23.5 us (6%)
  between operations  13.4 us (4%)
  starting transfers between devices  5.64 us (2%)
    all_to_all x1, waiting for transfers between devices, mirror_after(): lax.all_to_all(owned, 'row', split_axis=2, concat_axis=1, tiled=True)  115 us
    reduce_scatter x1, waiting for transfers between devices, reduce_pairs(): lax.psum_scatter(partial_sums, 'col', scatter_dimension=0, tiled=True)  101 us
    dot_general x1, matrix products, local(): jnp.dot(masked.reshape(pair_count, slab_width * d_width), integrals.resha...  79.4 us
    all_gather x1, blocking collectives, local(): gathered = lax.all_gather(amplitudes, 'row', axis=0, tiled=True)  32.6 us
    all_to_all x2, local copies, waits for them, and re-layouts, mirror_after(): lax.all_to_all(owned, 'row', split_axis=2, concat_axis=1, tiled=True)  13.4 us
  transfers between devices with their start and end apart: 2, of which 2 were waited for; matrix products, arithmetic and copies ran while one was open for 0% of the time, Pallas kernels for 0%

commit v1 on v0

--- a/solution.py
+++ b/solution.py
@@ -43,7 +43,10 @@
     full_width = integrals.shape[3]
     row_index = lax.axis_index("row")
     col_index = lax.axis_index("col")
-    gathered = lax.all_gather(amplitudes, "row", axis=0, tiled=True)
+    size = lax.axis_size("row")
+    pieces = jnp.stack([amplitudes for _ in range(size)])
+    pieces = lax.all_to_all(pieces, "row", split_axis=0, concat_axis=0)
+    gathered = jnp.concatenate(pieces, axis=0)
     pair_count = gathered.shape[0]
     c_labels = virt_irrep[:slab_width]
     d_labels = lax.dynamic_slice_in_dim(virt_irrep, col_index * d_width, d_width)

time: 376 us -> 354 us (0.941)
  blocking collectives: 32.6 us -> 0 us
  starting transfers between devices: 5.64 us -> 13 us
    all_gather x1 -> x0, blocking collectives: 32.6 us -> none  [local(): gathered = lax.all_gather(amplitudes, 'row', axis=0, tiled=True)]
    all_to_all x0 -> x1, starting transfers between devices: none -> 7.31 us  [local(): pieces = lax.all_to_all(pieces, 'row', split_axis=0, concat_axis=0)]
    all_to_all x0 -> x1, waiting for transfers between devices: none -> 3.96 us  [local(): pieces = lax.all_to_all(pieces, 'row', split_axis=0, concat_axis=0)]
  transfers between devices with their start and end apart: 2 -> 3, of which waited for: 2 -> 3; matrix products, arithmetic and copies ran while one was open for 0% -> 1% of each run, Pallas kernels for 0% -> 0%
where the time goes in v1:
time: 354 us; the launch traced here: 353 us
  waiting for transfers between devices  218 us (62%)
  matrix products  80.6 us (23%)
  local copies, waits for them, and re-layouts  25.6 us (7%)
  between operations  13.4 us (4%)
  starting transfers between devices  13 us (4%)
    all_to_all x1, waiting for transfers between devices, mirror_after(): lax.all_to_all(owned, 'row', split_axis=2, concat_axis=1, tiled=True)  115 us
    reduce_scatter x1, waiting for transfers between devices, reduce_pairs(): lax.psum_scatter(partial_sums, 'col', scatter_dimension=0, tiled=True)  98.3 us
    dot_general x1, matrix products, local(): jnp.dot(masked.reshape(pair_count, slab_width * d_width), integrals.resha...  79.5 us
    all_to_all x2, local copies, waits for them, and re-layouts, mirror_after(): lax.all_to_all(owned, 'row', split_axis=2, concat_axis=1, tiled=True)  13.4 us
    all_to_all x1, starting transfers between devices, local(): pieces = lax.all_to_all(pieces, 'row', split_axis=0, concat_axis=0)  7.31 us
  transfers between devices with their start and end apart: 3, of which 3 were waited for; matrix products, arithmetic and copies ran while one was open for 1% of the time, Pallas kernels for 0%

profile of v1, /device:TPU:0, one launch (start us, length us, event | category | flops | bytes accessed | tf_op | source)
XLA Modules:
  0.0 353.1 jit_solution(2218227761767054255)
XLA Ops:
  6.5 1.4 stack.2
  7.9 7.3 %all-to-all-start = ((f32[8,8,2,160]{3,2,1,0:T(2,128)}), f32[8,8,2,160]{3,2,1,0:T(2,128)S(1)}, u32[]{:S(2)}, u32[]{:S(2)}) async-start(f32[8,8,2,160]{3,2,1,0:T(2,128)} %stack.2), calls=%async_computation | async-start | bytes 262144 | tf_op jit(solution)/shard_map/all_to_all | solution.py:48
  15.3 0.0 reduce-scatter.2.cloned.1.call-start
  15.3 0.7 slice.3
  16.0 0.8 dynamic_slice.11
  16.8 0.7 eq.60
  17.5 0.9 fusion.6
  18.4 0.2 fusion.4
  18.6 0.1 broadcast_xor_fusion.1
  18.6 4.0 %all-to-all-done = f32[8,8,2,160]{3,2,1,0:T(2,128)S(1)} async-done(((f32[8,8,2,160]{3,2,1,0:T(2,128)}), f32[8,8,2,160]{3,2,1,0:T(2,128)S(1)}, u32[]{:S(2)}, u32[]{:S(2)}) %all-to-all-start) | async-done | bytes 81952 | tf_op jit(solution)/shard_map/all_to_all | solution.py:48
  22.6 0.1 compare_select_fusion
  22.7 0.1 reshape.89
  22.9 79.5 %fusion = f32[64,80,640]{2,0,1:T(8,128)} fusion(f32[64,320,1]{1,0,2:T(8,128)S(1)} %reshape.89, f32[40,8,80,640]{3,2,1,0:T(8,128)} %bitcast.26), kind=kOutput, calls=%fused_computation | convolution fusion | flops 12582912000 | bytes 78725120 | tf_op jit(solution)/shard_map/dot_general | solution.py:54
  102.4 0.0 reduce-scatter.2.cloned.1.call-update
  102.4 98.3 %reduce-scatter.2.cloned.1.call-done = f32[16,80,640]{2,0,1:T(8,128)} async-done(((f32[64,80,640]{2,0,1:T(8,128)}), f32[16,80,640]{2,0,1:T(8,128)}) %reduce-scatter.2.cloned.1.call-update) | async-done | bytes 3276816 | tf_op jit(solution)/shard_map/reduce_scatter | solution.py:8
  200.8 5.6 %copy.16 = f32[16,80,640]{1,0,2:T(8,128)} copy(f32[16,80,640]{2,0,1:T(8,128)} %reduce-scatter.2.cloned.1.call-done) | data formatting | bytes 6553600 | tf_op jit(solution)/shard_map/reduce_scatter | solution.py:8
  206.4 0.0 copy-start.2
  206.4 0.0 copy-start.1
  206.4 5.6 %all-to-all-start.1 = ((f32[16,80,640]{1,0,2:T(8,128)}), f32[16,80,640]{1,0,2:T(8,128)}, u32[]{:S(2)}, u32[]{:S(2)}) async-start(f32[16,80,640]{1,0,2:T(8,128)} %copy.16), calls=%async_computation.2 | async-start | bytes 10485760 | tf_op jit(solution)/shard_map/all_to_all | solution.py:12
  212.1 0.0 copy-done.2
  212.1 0.1 dynamic_slice.10
  212.1 0.0 copy-done.1
  212.1 0.1 dynamic_slice.9
  212.2 0.1 broadcast_xor_fusion
  212.3 115.3 %all-to-all-done.1 = f32[16,80,640]{1,0,2:T(8,128)} async-done(((f32[16,80,640]{1,0,2:T(8,128)}), f32[16,80,640]{1,0,2:T(8,128)}, u32[]{:S(2)}, u32[]{:S(2)}) %all-to-all-start.1) | async-done | bytes 3276832 | tf_op jit(solution)/shard_map/all_to_all | solution.py:12
  327.7 7.8 %copy.29 = f32[16,80,8,80]{1,2,0,3:T(8,128)} copy(f32[16,80,8,80]{1,0,3,2:T(8,128)} %bitcast.1) | data formatting | bytes 6553600 | tf_op jit(solution)/shard_map/all_to_all | solution.py:12
  335.5 0.0 copy-start
  335.5 5.5 %all_to_all.20 = f32[16,640,80]{1,0,2:T(8,128)} reshape(f32[16,8,80,80]{2,1,0,3:T(8,128)} %bitcast.27) | data formatting | bytes 6553600 | tf_op jit(solution)/shard_map/all_to_all | solution.py:12
  341.0 0.0 copy-done
  341.0 2.5 fusion.3
  343.6 2.7 copy.18
Async XLA Ops:
  7.9 14.7 %all-to-all-start = ((f32[8,8,2,160]{3,2,1,0:T(2,128)}), f32[8,8,2,160]{3,2,1,0:T(2,128)S(1)}, u32[]{:S(2)}, u32[]{:S(2)}) async-start(f32[8,8,2,160]{3,2,1,0:T(2,128)} %stack.2), calls=%async_computation | async-start | bytes 262144 | tf_op jit(solution)/shard_map/all_to_all | solution.py:48
  15.3 185.5 %reduce-scatter.2.cloned.1.call-start = ((), (), s32[]{:S(2)}) async-start(), calls=%async_computation.3 | async-start | bytes 16384000 | tf_op jit(solution)/shard_map/reduce_scatter | solution.py:8
  206.4 5.7 %copy-start.2 = (s32[64]{0:T(128)S(1)}, s32[64]{0:T(128)}, u32[]{:S(2)}) copy-start(s32[64]{0:T(128)} %param.8) | copy-start | bytes 772
  206.4 5.7 %copy-start.1 = (s32[640]{0:T(1024)S(1)}, s32[640]{0:T(1024)}, u32[]{:S(2)}) copy-start(s32[640]{0:T(1024)} %param.7) | copy-start | bytes 7684
  206.4 121.2 %all-to-all-start.1 = ((f32[16,80,640]{1,0,2:T(8,128)}), f32[16,80,640]{1,0,2:T(8,128)}, u32[]{:S(2)}, u32[]{:S(2)}) async-start(f32[16,80,640]{1,0,2:T(8,128)} %copy.16), calls=%async_computation.2 | async-start | bytes 10485760 | tf_op jit(solution)/shard_map/all_to_all | solution.py:12
  335.5 5.5 %copy-start = (f32[16,80,640]{2,0,1:T(8,128)S(1)}, f32[16,80,640]{2,0,1:T(8,128)}, u32[]{:S(2)}) copy-start(f32[16,80,640]{2,0,1:T(8,128)} %reduce-scatter.2.cloned.1.call-done) | copy-start | bytes 9830404
Sparse Core Ops, SparseCore 0:
  102.6 98.1 reduce-scatter.1
